TPU v7x, 32 devices: a whole 2x2x4 slice. The times are simulated.
32 devices in a mesh: section: 4 (over y, x), frame: 4 (over z), row: 2 (over core).
Axes of the slice: x: 2, y: 2, z: 4, core: 2. Of those that a mesh axis runs over, the one named last changes fastest.
Arguments:
- x_saved: bfloat16 [4, 8, 16, 64, 128], P('section', 'frame', 'row'), may hold values from -6 to 6
- cotangent: bfloat16 [8, 16, 64, 128], P('frame', 'row'), may hold values from -6 to 6
- w_spatial: bfloat16 [4, 3, 3, 128, 128], P('section'), may hold values from -0.1875 to 0.1875
- w_temporal: bfloat16 [4, 3, 128, 128], P('section'), may hold values from -0.3125 to 0.3125
Outputs:
- grad_inputs: bfloat16 [4, 8, 16, 64, 128], P('section', 'frame', 'row')
- grad_spatial: float32 [4, 3, 3, 128, 128], P('section')
- grad_temporal: float32 [4, 3, 128, 128], P('section')
All inputs are finite; a program needn't handle non-finite values.
Results may differ from a plain program's by a relative error of at most 0.014.
Values may be sent and summed in bfloat16 or wider, within the bound.
No kernel may reach another device: no remote copies, remote signals or barrier semaphores. Data moves between devices by JAX's collectives and lax.ppermute only.
A program may use at most 64 MiB of HBM per device.

v0:
```python
import jax
import jax.numpy as jnp
from jax import lax
from jax.sharding import PartitionSpec as P


def padded_2(cells, sides, width):
    for axis, dim in sides:
        count = lax.axis_size(axis)
        ends = count - 1
        head = lax.slice_in_dim(cells, 0, width, axis=dim)
        tail = lax.slice_in_dim(cells, cells.shape[dim] - width, cells.shape[dim], axis=dim)
        cells = jnp.concatenate(
            [
                lax.ppermute(tail, axis, [(i, (i + 1) % count) for i in range(ends)]),
                cells,
                lax.ppermute(head, axis, [((i + 1) % count, i) for i in range(ends)]),
            ],
            axis=dim,
        )
    return cells


def from_behind(block, axis, distance):
    devices = range(lax.axis_size(axis))
    route = [(i - distance, i) for i in devices if i - distance in devices]
    return lax.ppermute(block, axis, route)


def slope_of(pre_act):
    sigma = jax.nn.sigmoid(pre_act)
    return sigma * (1.0 + pre_act * (1.0 - sigma))


def inner_sum(first_arg, second_arg):
    return lax.dot_general(
        first_arg, second_arg, (((0,), (0,)), ((), ())), preferred_element_type=jnp.float32
    )


def pad_cols(values):
    return jnp.pad(values, ((0, 0), (0, 0), (1, 1), (0, 0)))


def frame_shift(values, offset, max_reach):
    widths = [(max_reach, max_reach)] + [(0, 0)] * (values.ndim - 1)
    padded = jnp.pad(values, widths)
    return lax.dynamic_slice_in_dim(padded, max_reach + offset, values.shape[0], 0)


def apply_taps(padded, taps, row_count, col_count, transpose):
    channels = padded.shape[-1]
    running = jnp.zeros((padded.shape[0] * row_count * col_count, taps.shape[-1]), jnp.float32)
    for i in range(3):
        for j in range(3):
            window = padded[:, i : i + row_count, j : j + col_count, :].reshape(-1, channels)
            if transpose:
                running = running + jnp.dot(
                    window, taps[2 - i, 2 - j].T, preferred_element_type=jnp.float32
                )
            else:
                running = running + jnp.dot(window, taps[i, j], preferred_element_type=jnp.float32)
    return running.reshape(padded.shape[0], row_count, col_count, taps.shape[-1])


def to_blocks(values, frame_parts):
    frame_count, row_count, col_count, channels = values.shape
    return values.reshape(frame_count, frame_parts, row_count * col_count // frame_parts, channels)


def temporal_back(segment, taps_time, dilation, max_reach):
    channels = segment.shape[-1]
    running = jnp.zeros((segment.size // channels, channels), jnp.float32)
    for k in range(3):
        shifted = frame_shift(segment, (1 - k) * dilation, max_reach).reshape(-1, channels)
        running = running + jnp.dot(shifted, taps_time[k].T, preferred_element_type=jnp.float32)
    return running.astype(jnp.bfloat16).reshape(segment.shape)


def spatial_back(back_tiles, pre_slope, taps_space, local_shape):
    back_act = lax.all_to_all(back_tiles, "frame", split_axis=0, concat_axis=1, tiled=True).reshape(
        local_shape
    )
    grad_pre = (back_act.astype(jnp.float32) * pre_slope).astype(jnp.bfloat16)
    rims = padded_2(grad_pre, (("row", 1),), 1)
    branch = apply_taps(pad_cols(rims), taps_space, local_shape[1], local_shape[2], True).astype(
        jnp.bfloat16
    )
    return (grad_pre, branch)


def pass_back(outgoing):
    return from_behind(outgoing, "section", -1)


def section_run(x_saved, cotangent, w_spatial, w_temporal):
    block_input = x_saved[0]
    taps_space = w_spatial[0]
    taps_time = w_temporal[0]
    local_shape = block_input.shape
    row_count = local_shape[1]
    col_count = local_shape[2]
    channels = local_shape[3]
    frame_parts = lax.axis_size("frame")
    section_count = lax.axis_size("section")
    section_index = lax.axis_index("section")
    dilation = jnp.left_shift(jnp.int32(1), section_index)
    max_reach = 2 ** (section_count - 1)
    extended = pad_cols(padded_2(block_input, (("row", 1),), 1))
    pre_act = apply_taps(extended, taps_space, row_count, col_count, False)
    pre_slope = slope_of(pre_act)
    active = jax.nn.silu(pre_act).astype(jnp.bfloat16)
    active_tiles = lax.all_to_all(
        to_blocks(active, frame_parts), "frame", split_axis=1, concat_axis=0, tiled=True
    )
    kept_pre = jnp.zeros(local_shape, jnp.bfloat16)
    kept_tiles = jnp.zeros_like(active_tiles)
    incoming = cotangent
    own_grad = jnp.zeros(local_shape, jnp.bfloat16)
    for position in range(section_count):
        with_segment = lax.all_to_all(
            to_blocks(incoming, frame_parts), "frame", split_axis=1, concat_axis=0, tiled=True
        )
        back_tiles = temporal_back(with_segment, taps_time, dilation, max_reach)
        grad_pre, branch = spatial_back(back_tiles, pre_slope, taps_space, local_shape)
        outgoing = (
            incoming.astype(jnp.float32) + lax.optimization_barrier(branch).astype(jnp.float32)
        ).astype(jnp.bfloat16)
        is_owner = section_index == section_count - 1 - position
        own_grad = jnp.where(is_owner, outgoing, own_grad)
        kept_pre = jnp.where(is_owner, grad_pre, kept_pre)
        kept_tiles = jnp.where(is_owner, with_segment, kept_tiles)
        if position + 1 < section_count:
            incoming = pass_back(outgoing)
    flat_pre = kept_pre.reshape(-1, channels)
    grads_space = jnp.stack(
        [
            jnp.stack(
                [
                    inner_sum(
                        extended[:, i : i + row_count, j : j + col_count, :].reshape(-1, channels),
                        flat_pre,
                    )
                    for j in range(3)
                ]
            )
            for i in range(3)
        ]
    )
    flat_tiles = kept_tiles.reshape(-1, channels)
    grads_time = jnp.stack(
        [
            inner_sum(
                frame_shift(active_tiles, (k - 1) * dilation, max_reach).reshape(-1, channels),
                flat_tiles,
            )
            for k in range(3)
        ]
    )
    grads_space, grads_time = lax.psum((grads_space, grads_time), ("frame", "row"))
    return (own_grad[None], grads_space[None], grads_time[None])


def local(x_saved, cotangent, w_spatial, w_temporal):
    return section_run(x_saved, cotangent, w_spatial, w_temporal)


def solution(mesh):
    return jax.shard_map(
        local,
        mesh=mesh,
        in_specs=(
            P("section", "frame", "row", None, None),
            P("frame", "row", None, None),
            P("section", None, None, None, None),
            P("section", None, None, None),
        ),
        out_specs=(
            P("section", "frame", "row", None, None),
            P("section", None, None, None, None),
            P("section", None, None, None),
        ),
        check_vma=False,
    )
```

profile of v0, /device:TPU:0, one launch (start us, length us, event | category | flops | bytes accessed | tf_op | source)
XLA Modules:
  0.0 260.1 jit_solution(2147495361420427421)
XLA Ops:
  8.0 2.3 collective-permute-start
  11.6 1.7 copy.56
  13.3 5.8 %all-to-all-start = ((bf16[2,4,128,128]{3,2,0,1:T(8,128)(2,1)}), bf16[2,4,128,128]{3,2,0,1:T(8,128)(2,1)S(1)}, u32[]{:S(2)}, u32[]{:S(2)}) async-start(bf16[2,4,128,128]{3,2,0,1:T(8,128)(2,1)} %copy.56), calls=%async_computation | async-start | bytes 524288 | tf_op jit(solution)/shard_map/all_to_all | solution.py:121
  22.3 7.0 %all-to-all-done = bf16[2,4,128,128]{3,2,0,1:T(8,128)(2,1)S(1)} async-done(((bf16[2,4,128,128]{3,2,0,1:T(8,128)(2,1)}), bf16[2,4,128,128]{3,2,0,1:T(8,128)(2,1)S(1)}, u32[]{:S(2)}, u32[]{:S(2)}) %all-to-all-start) | async-done | bytes 262176 | tf_op jit(solution)/shard_map/all_to_all | solution.py:121
  31.6 3.4 %all-to-all-start.1 = ((bf16[8,1,128,128]{3,2,1,0:T(8,128)(2,1)}), bf16[8,1,128,128]{3,2,1,0:T(8,128)(2,1)S(1)}, u32[]{:S(2)}, u32[]{:S(2)}) async-start(bf16[8,1,128,128]{3,2,1,0:T(8,128)(2,1)} %bitcast.12), calls=%async_computation.1 | async-start | bytes 524288 | tf_op jit(solution)/shard_map/all_to_all | solution.py:81
  36.2 8.1 %all-to-all-done.1 = bf16[8,1,128,128]{3,2,1,0:T(8,128)(2,1)S(1)} async-done(((bf16[8,1,128,128]{3,2,1,0:T(8,128)(2,1)}), bf16[8,1,128,128]{3,2,1,0:T(8,128)(2,1)S(1)}, u32[]{:S(2)}, u32[]{:S(2)}) %all-to-all-start.1) | async-done | bytes 262176 | tf_op jit(solution)/shard_map/all_to_all | solution.py:81
  49.3 1.8 collective-permute-done.3
  55.8 9.0 %collective-permute-done.4 = bf16[2,8,64,128]{3,2,1,0:T(8,128)(2,1)S(1)} collective-permute-done((bf16[2,8,64,128]{3,2,1,0:T(8,128)(2,1)S(1)}, bf16[2,8,64,128]{3,2,1,0:T(8,128)(2,1)S(1)}, u32[]{:S(2)}, u32[]{:S(2)}) %collective-permute-start.4) | collective-permute-done | bytes 262176 | tf_op jit(solution)/shard_map/ppermute | solution.py:27
  64.8 11.1 %all_to_all.126 = bf16[2,4,128,128]{3,2,0,1:T(8,128)(2,1)S(1)} all-to-all(bf16[2,4,128,128]{3,2,0,1:T(8,128)(2,1)S(1)} %copy.61), channel_id=1, replica_groups=mesh['section'=4,'frame'=4,'row'=2] {'frame'}, dimensions={1} | all-to-all | bytes 524288 | tf_op jit(solution)/shard_map/all_to_all | solution.py:121
  76.7 10.9 %all_to_all.127 = bf16[8,1,128,128]{3,2,1,0:T(8,128)(2,1)S(1)} all-to-all(bf16[8,1,128,128]{3,2,1,0:T(8,128)(2,1)S(1)} %bitcast.560), channel_id=1, replica_groups=mesh['section'=4,'frame'=4,'row'=2] {'frame'}, dimensions={0} | all-to-all | bytes 524288 | tf_op jit(solution)/shard_map/all_to_all | solution.py:81
  91.4 1.6 collective-permute-done.6
  96.9 9.6 %collective-permute-done.7 = bf16[2,8,64,128]{3,2,1,0:T(8,128)(2,1)S(1)} collective-permute-done((bf16[2,8,64,128]{3,2,1,0:T(8,128)(2,1)S(1)}, bf16[2,8,64,128]{3,2,1,0:T(8,128)(2,1)S(1)}, u32[]{:S(2)}, u32[]{:S(2)}) %collective-permute-start.7) | collective-permute-done | bytes 262176 | tf_op jit(solution)/shard_map/ppermute | solution.py:27
  106.5 11.3 %all_to_all.128 = bf16[2,4,128,128]{3,2,0,1:T(8,128)(2,1)S(1)} all-to-all(bf16[2,4,128,128]{3,2,0,1:T(8,128)(2,1)S(1)} %copy.66), channel_id=1, replica_groups=mesh['section'=4,'frame'=4,'row'=2] {'frame'}, dimensions={1} | all-to-all | bytes 524288 | tf_op jit(solution)/shard_map/all_to_all | solution.py:121
  118.7 10.9 %all_to_all.129 = bf16[8,1,128,128]{3,2,1,0:T(8,128)(2,1)S(1)} all-to-all(bf16[8,1,128,128]{3,2,1,0:T(8,128)(2,1)S(1)} %bitcast.561), channel_id=1, replica_groups=mesh['section'=4,'frame'=4,'row'=2] {'frame'}, dimensions={0} | all-to-all | bytes 524288 | tf_op jit(solution)/shard_map/all_to_all | solution.py:81
  139.6 9.6 %collective-permute-done.10 = bf16[2,8,64,128]{3,2,1,0:T(8,128)(2,1)S(1)} collective-permute-done((bf16[2,8,64,128]{3,2,1,0:T(8,128)(2,1)S(1)}, bf16[2,8,64,128]{3,2,1,0:T(8,128)(2,1)S(1)}, u32[]{:S(2)}, u32[]{:S(2)}) %collective-permute-start.10) | collective-permute-done | bytes 262176 | tf_op jit(solution)/shard_map/ppermute | solution.py:27
  150.0 3.4 %all-to-all-start.6 = ((bf16[2,4,128,128]{3,2,0,1:T(8,128)(2,1)}), bf16[2,4,128,128]{3,2,0,1:T(8,128)(2,1)S(1)}, u32[]{:S(2)}, u32[]{:S(2)}) async-start(bf16[2,4,128,128]{3,2,0,1:T(8,128)(2,1)} %copy.71), calls=%async_computation.6 | async-start | bytes 524288 | tf_op jit(solution)/shard_map/all_to_all | solution.py:121
  154.5 1.9 multiply_convert_fusion
  156.4 6.1 %all-to-all-done.6 = bf16[2,4,128,128]{3,2,0,1:T(8,128)(2,1)S(1)} async-done(((bf16[2,4,128,128]{3,2,0,1:T(8,128)(2,1)}), bf16[2,4,128,128]{3,2,0,1:T(8,128)(2,1)S(1)}, u32[]{:S(2)}, u32[]{:S(2)}) %all-to-all-start.6) | async-done | bytes 262176 | tf_op jit(solution)/shard_map/all_to_all | solution.py:121
  162.4 4.1 %all-to-all-start.8 = ((bf16[2,4,128,128]{2,3,0,1:T(8,128)(2,1)}), bf16[2,4,128,128]{2,3,0,1:T(8,128)(2,1)}, u32[]{:S(2)}, u32[]{:S(2)}) async-start(bf16[2,4,128,128]{2,3,0,1:T(8,128)(2,1)} %multiply_convert_fusion), calls=%async_computation.8 | async-start | bytes 524288 | tf_op jit(solution)/shard_map/all_to_all | solution.py:113
  168.1 5.4 %all-to-all-done.8 = bf16[2,4,128,128]{2,3,0,1:T(8,128)(2,1)} async-done(((bf16[2,4,128,128]{2,3,0,1:T(8,128)(2,1)}), bf16[2,4,128,128]{2,3,0,1:T(8,128)(2,1)}, u32[]{:S(2)}, u32[]{:S(2)}) %all-to-all-start.8) | async-done | bytes 262176 | tf_op jit(solution)/shard_map/all_to_all | solution.py:113
  173.5 3.4 %all-to-all-start.7 = ((bf16[8,1,128,128]{3,2,1,0:T(8,128)(2,1)}), bf16[8,1,128,128]{3,2,1,0:T(8,128)(2,1)S(1)}, u32[]{:S(2)}, u32[]{:S(2)}) async-start(bf16[8,1,128,128]{3,2,1,0:T(8,128)(2,1)} %bitcast.550), calls=%async_computation.7 | async-start | bytes 524288 | tf_op jit(solution)/shard_map/all_to_all | solution.py:81
  181.4 2.3 all-to-all-done.7
  196.8 53.8 %all-reduce.13.cloned.1.call-done = (f32[1,3,3,128,128]{4,3,2,1,0:T(8,128)}, f32[1,3,128,128]{3,2,1,0:T(8,128)}) async-done(((f32[1,3,3,128,128]{4,3,2,1,0:T(8,128)}, f32[1,3,128,128]{3,2,1,0:T(8,128)}), (f32[1,3,3,128,128]{4,3,2,1,0:T(8,128)}, f32[1,3,128,128]{3,2,1,0:T(8,128)})) %all-reduce.13.cloned.1.call-update) | async-done | bytes 786448 | tf_op jit(solution)/shard_map/psum | solution.py:160
  250.6 2.0 copy.98
  (196 shorter events, 58.6 us)
Async XLA Ops:
  8.0 11.2 %collective-permute-start = (bf16[2,1,64,128]{3,2,1,0:T(8,128)(2,1)S(1)}, bf16[2,1,64,128]{3,2,1,0:T(8,128)(2,1)S(1)}, u32[]{:S(2)}, u32[]{:S(2)}) collective-permute-start(bf16[2,1,64,128]{3,2,1,0:T(8,128)(2,1)S(1)} %get-tuple-element.61), channel_id=1, source_target_pairs={{0,1},{2,3},{4,5},{6,7},{8,9},{10,11},{12,13},{14,15},{16,17},{18,... | collective-permute-start | bytes 98312 | tf_op jit(solution)/shard_map/ppermute | solution.py:15
  10.3 8.8 %collective-permute-start.1 = (bf16[2,1,64,128]{3,2,1,0:T(8,128)(2,1)S(1)}, bf16[2,1,64,128]{3,2,1,0:T(8,128)(2,1)S(1)}, u32[]{:S(2)}, u32[]{:S(2)}) collective-permute-start(bf16[2,1,64,128]{3,2,1,0:T(8,128)(2,1)S(1)} %get-tuple-element.62), channel_id=1, source_target_pairs={{1,0},{3,2},{5,4},{7,6},{9,8},{11,10},{13,12},{15,14},{17,16},{19,... | collective-permute-start | bytes 98312 | tf_op jit(solution)/shard_map/ppermute | solution.py:17
  13.3 5.8 %copy-start.1 = (bf16[1,2,8,64,128]{4,3,2,1,0:T(8,128)(2,1)S(1)}, bf16[1,2,8,64,128]{4,3,2,1,0:T(8,128)(2,1)}, u32[]{:S(2)}) copy-start(bf16[1,2,8,64,128]{4,3,2,1,0:T(8,128)(2,1)} %param.4) | copy-start | bytes 786436
  13.3 16.0 %all-to-all-start = ((bf16[2,4,128,128]{3,2,0,1:T(8,128)(2,1)}), bf16[2,4,128,128]{3,2,0,1:T(8,128)(2,1)S(1)}, u32[]{:S(2)}, u32[]{:S(2)}) async-start(bf16[2,4,128,128]{3,2,0,1:T(8,128)(2,1)} %copy.56), calls=%async_computation | async-start | bytes 524288 | tf_op jit(solution)/shard_map/all_to_all | solution.py:121
  31.6 12.7 %all-to-all-start.1 = ((bf16[8,1,128,128]{3,2,1,0:T(8,128)(2,1)}), bf16[8,1,128,128]{3,2,1,0:T(8,128)(2,1)S(1)}, u32[]{:S(2)}, u32[]{:S(2)}) async-start(bf16[8,1,128,128]{3,2,1,0:T(8,128)(2,1)} %bitcast.12), calls=%async_computation.1 | async-start | bytes 524288 | tf_op jit(solution)/shard_map/all_to_all | solution.py:81
  46.7 2.6 %collective-permute-start.2 = (bf16[2,1,64,128]{3,2,1,0:T(8,128)(2,1)S(1)}, bf16[2,1,64,128]{3,2,1,0:T(8,128)(2,1)S(1)}, u32[]{:S(2)}, u32[]{:S(2)}) collective-permute-start(bf16[2,1,64,128]{3,2,1,0:T(8,128)(2,1)S(1)} %get-tuple-element.57), channel_id=1, source_target_pairs={{0,1},{2,3},{4,5},{6,7},{8,9},{10,11},{12,13},{14,15},{16,17},{18,... | collective-permute-start | bytes 98312 | tf_op jit(solution)/shard_map/ppermute | solution.py:15
  48.0 3.1 %collective-permute-start.3 = (bf16[2,1,64,128]{3,2,1,0:T(8,128)(2,1)S(1)}, bf16[2,1,64,128]{3,2,1,0:T(8,128)(2,1)S(1)}, u32[]{:S(2)}, u32[]{:S(2)}) collective-permute-start(bf16[2,1,64,128]{3,2,1,0:T(8,128)(2,1)S(1)} %get-tuple-element.58), channel_id=1, source_target_pairs={{1,0},{3,2},{5,4},{7,6},{9,8},{11,10},{13,12},{15,14},{17,16},{19,... | collective-permute-start | bytes 98312 | tf_op jit(solution)/shard_map/ppermute | solution.py:17
  54.5 10.3 %copy-start.10 = (bf16[2,8,64,128]{3,2,1,0:T(8,128)(2,1)}, bf16[2,8,64,128]{3,2,1,0:T(8,128)(2,1)S(1)}, u32[]{:S(2)}) copy-start(bf16[2,8,64,128]{3,2,1,0:T(8,128)(2,1)S(1)} %add_convert_fusion.3) | copy-start | bytes 786436
  54.5 10.3 %collective-permute-start.4 = (bf16[2,8,64,128]{3,2,1,0:T(8,128)(2,1)S(1)}, bf16[2,8,64,128]{3,2,1,0:T(8,128)(2,1)S(1)}, u32[]{:S(2)}, u32[]{:S(2)}) collective-permute-start(bf16[2,8,64,128]{3,2,1,0:T(8,128)(2,1)S(1)} %add_convert_fusion.3), channel_id=1, source_target_pairs={{8,0},{16,8},{24,16},{9,1},{17,9},{25,17},{10,2},{18,10},{26,18},{... | collective-permute-start | bytes 786440 | tf_op jit(solution)/shard_map/ppermute | solution.py:27
  88.6 2.8 %collective-permute-start.5 = (bf16[2,1,64,128]{3,2,1,0:T(8,128)(2,1)S(1)}, bf16[2,1,64,128]{3,2,1,0:T(8,128)(2,1)S(1)}, u32[]{:S(2)}, u32[]{:S(2)}) collective-permute-start(bf16[2,1,64,128]{3,2,1,0:T(8,128)(2,1)S(1)} %get-tuple-element.51), channel_id=1, source_target_pairs={{0,1},{2,3},{4,5},{6,7},{8,9},{10,11},{12,13},{14,15},{16,17},{18,... | collective-permute-start | bytes 98312 | tf_op jit(solution)/shard_map/ppermute | solution.py:15
  89.9 3.1 %collective-permute-start.6 = (bf16[2,1,64,128]{3,2,1,0:T(8,128)(2,1)S(1)}, bf16[2,1,64,128]{3,2,1,0:T(8,128)(2,1)S(1)}, u32[]{:S(2)}, u32[]{:S(2)}) collective-permute-start(bf16[2,1,64,128]{3,2,1,0:T(8,128)(2,1)S(1)} %get-tuple-element.52), channel_id=1, source_target_pairs={{1,0},{3,2},{5,4},{7,6},{9,8},{11,10},{13,12},{15,14},{17,16},{19,... | collective-permute-start | bytes 98312 | tf_op jit(solution)/shard_map/ppermute | solution.py:17
  95.6 10.9 %copy-start.12 = (bf16[2,8,64,128]{3,2,1,0:T(8,128)(2,1)}, bf16[2,8,64,128]{3,2,1,0:T(8,128)(2,1)S(1)}, u32[]{:S(2)}) copy-start(bf16[2,8,64,128]{3,2,1,0:T(8,128)(2,1)S(1)} %add_convert_fusion.2) | copy-start | bytes 786436
  95.6 10.9 %collective-permute-start.7 = (bf16[2,8,64,128]{3,2,1,0:T(8,128)(2,1)S(1)}, bf16[2,8,64,128]{3,2,1,0:T(8,128)(2,1)S(1)}, u32[]{:S(2)}, u32[]{:S(2)}) collective-permute-start(bf16[2,8,64,128]{3,2,1,0:T(8,128)(2,1)S(1)} %add_convert_fusion.2), channel_id=1, source_target_pairs={{8,0},{16,8},{24,16},{9,1},{17,9},{25,17},{10,2},{18,10},{26,18},{... | collective-permute-start | bytes 786440 | tf_op jit(solution)/shard_map/ppermute | solution.py:27
  130.6 2.8 %collective-permute-start.8 = (bf16[2,1,64,128]{3,2,1,0:T(8,128)(2,1)S(1)}, bf16[2,1,64,128]{3,2,1,0:T(8,128)(2,1)S(1)}, u32[]{:S(2)}, u32[]{:S(2)}) collective-permute-start(bf16[2,1,64,128]{3,2,1,0:T(8,128)(2,1)S(1)} %get-tuple-element.45), channel_id=1, source_target_pairs={{0,1},{2,3},{4,5},{6,7},{8,9},{10,11},{12,13},{14,15},{16,17},{18,... | collective-permute-start | bytes 98312 | tf_op jit(solution)/shard_map/ppermute | solution.py:15
  131.9 3.1 %collective-permute-start.9 = (bf16[2,1,64,128]{3,2,1,0:T(8,128)(2,1)S(1)}, bf16[2,1,64,128]{3,2,1,0:T(8,128)(2,1)S(1)}, u32[]{:S(2)}, u32[]{:S(2)}) collective-permute-start(bf16[2,1,64,128]{3,2,1,0:T(8,128)(2,1)S(1)} %get-tuple-element.46), channel_id=1, source_target_pairs={{1,0},{3,2},{5,4},{7,6},{9,8},{11,10},{13,12},{15,14},{17,16},{19,... | collective-permute-start | bytes 98312 | tf_op jit(solution)/shard_map/ppermute | solution.py:17
  138.4 10.9 %collective-permute-start.10 = (bf16[2,8,64,128]{3,2,1,0:T(8,128)(2,1)S(1)}, bf16[2,8,64,128]{3,2,1,0:T(8,128)(2,1)S(1)}, u32[]{:S(2)}, u32[]{:S(2)}) collective-permute-start(bf16[2,8,64,128]{3,2,1,0:T(8,128)(2,1)S(1)} %add_convert_fusion.1), channel_id=1, source_target_pairs={{8,0},{16,8},{24,16},{9,1},{17,9},{25,17},{10,2},{18,10},{26,18},{... | collective-permute-start | bytes 786440 | tf_op jit(solution)/shard_map/ppermute | solution.py:27
  150.0 12.4 %all-to-all-start.6 = ((bf16[2,4,128,128]{3,2,0,1:T(8,128)(2,1)}), bf16[2,4,128,128]{3,2,0,1:T(8,128)(2,1)S(1)}, u32[]{:S(2)}, u32[]{:S(2)}) async-start(bf16[2,4,128,128]{3,2,0,1:T(8,128)(2,1)} %copy.71), calls=%async_computation.6 | async-start | bytes 524288 | tf_op jit(solution)/shard_map/all_to_all | solution.py:121
  162.4 11.1 %all-to-all-start.8 = ((bf16[2,4,128,128]{2,3,0,1:T(8,128)(2,1)}), bf16[2,4,128,128]{2,3,0,1:T(8,128)(2,1)}, u32[]{:S(2)}, u32[]{:S(2)}) async-start(bf16[2,4,128,128]{2,3,0,1:T(8,128)(2,1)} %multiply_convert_fusion), calls=%async_computation.8 | async-start | bytes 524288 | tf_op jit(solution)/shard_map/all_to_all | solution.py:113
  173.5 10.2 %all-to-all-start.7 = ((bf16[8,1,128,128]{3,2,1,0:T(8,128)(2,1)}), bf16[8,1,128,128]{3,2,1,0:T(8,128)(2,1)S(1)}, u32[]{:S(2)}, u32[]{:S(2)}) async-start(bf16[8,1,128,128]{3,2,1,0:T(8,128)(2,1)} %bitcast.550), calls=%async_computation.7 | async-start | bytes 524288 | tf_op jit(solution)/shard_map/all_to_all | solution.py:81
  176.9 73.7 %all-reduce.13.cloned.1.call-start = ((), (), s32[]{:S(2)}) async-start(), calls=%async_computation.9 | async-start | bytes 1572864 | tf_op jit(solution)/shard_map/psum | solution.py:160
  187.6 2.6 %copy-start.24 = (bf16[2,1,64,128]{3,2,1,0:T(8,128)(2,1)S(1)}, bf16[2,1,64,128]{3,2,1,0:T(8,128)(2,1)}, u32[]{:S(2)}) copy-start(bf16[2,1,64,128]{3,2,1,0:T(8,128)(2,1)} %copy-done.23) | copy-start | bytes 98308
  187.6 4.9 %collective-permute-start.11 = (bf16[2,1,64,128]{3,2,1,0:T(8,128)(2,1)S(1)}, bf16[2,1,64,128]{3,2,1,0:T(8,128)(2,1)S(1)}, u32[]{:S(2)}, u32[]{:S(2)}) collective-permute-start(bf16[2,1,64,128]{3,2,1,0:T(8,128)(2,1)S(1)} %get-tuple-element.39), channel_id=1, source_target_pairs={{0,1},{2,3},{4,5},{6,7},{8,9},{10,11},{12,13},{14,15},{16,17},{18,... | collective-permute-start | bytes 98312 | tf_op jit(solution)/shard_map/ppermute | solution.py:15
  188.9 3.6 %collective-permute-start.12 = (bf16[2,1,64,128]{3,2,1,0:T(8,128)(2,1)S(1)}, bf16[2,1,64,128]{3,2,1,0:T(8,128)(2,1)S(1)}, u32[]{:S(2)}, u32[]{:S(2)}) collective-permute-start(bf16[2,1,64,128]{3,2,1,0:T(8,128)(2,1)S(1)} %get-tuple-element.40), channel_id=1, source_target_pairs={{1,0},{3,2},{5,4},{7,6},{9,8},{11,10},{13,12},{15,14},{17,16},{19,... | collective-permute-start | bytes 98312 | tf_op jit(solution)/shard_map/ppermute | solution.py:17
  250.6 2.0 copy-start.20
  (20 other events, 19.3 us)
Sparse Core Ops, SparseCore 0:
  192.6 57.9 all-reduce.12
where the time goes:
time: 262 us; the launch traced here: 260 us
  waiting for transfers between devices  116 us (44%)
  blocking collectives  44.2 us (17%)
  starting transfers between devices  38.2 us (15%)
  matrix products  21.1 us (8%)
  local copies, waits for them, and re-layouts  17.5 us (7%)
  between operations  15.1 us (6%)
  other arithmetic  8.21 us (3%)
    psum x1, waiting for transfers between devices, section_run(): lax.psum((grads_space, grads_time), ('frame', 'row'))  53.8 us
    ppermute x3, waiting for transfers between devices, from_behind(): return lax.ppermute(block, axis, route)  28.2 us
    all_to_all x2, blocking collectives, section_run(): lax.all_to_all(to_blocks(incoming, frame_parts), 'frame', split_axis=1, c...  22.4 us
    all_to_all x2, blocking collectives, spatial_back(): lax.all_to_all(back_tiles, 'frame', split_axis=0, concat_axis=1, tiled=True)  21.8 us
    all_to_all x2, waiting for transfers between devices, section_run(): lax.all_to_all(to_blocks(incoming, frame_parts), 'frame', split_axis=1, c...  13.1 us
    unnamed x52, local copies, waits for them, and re-layouts  11.2 us
    all_to_all x2, waiting for transfers between devices, spatial_back(): lax.all_to_all(back_tiles, 'frame', split_axis=0, concat_axis=1, tiled=True)  10.4 us
    all_to_all x2, starting transfers between devices, section_run(): lax.all_to_all(to_blocks(incoming, frame_parts), 'frame', split_axis=1, c...  9.24 us
  transfers between devices with their start and end apart: 19, of which 12 were waited for; matrix products, arithmetic and copies ran while one was open for 7% of the time, Pallas kernels for 0%

commit v1 on v0

--- a/solution.py
+++ b/solution.py
@@ -157,7 +157,7 @@
             for k in range(3)
         ]
     )
-    grads_space, grads_time = lax.psum((grads_space, grads_time), ("frame", "row"))
+    grads_space, grads_time = lax.psum(lax.psum((grads_space, grads_time), "row"), "frame")
     return (own_grad[None], grads_space[None], grads_time[None])
 
 

time: 262 us -> 271 us (1.034)
  waiting for transfers between devices: 116 us -> 125 us
    psum x1 -> x2, waiting for transfers between devices: 53.8 us -> 63.3 us  [the longest x1 45.6 us: section_run(): lax.psum(lax.psum((grads_space, grads_time), 'row'), 'frame')]
  transfers between devices with their start and end apart: 19 -> 20, of which waited for: 12 -> 13; matrix products, arithmetic and copies ran while one was open for 7% -> 7% of each run, Pallas kernels for 0% -> 0%
where the time goes in v1:
time: 271 us; the launch traced here: 270 us
  waiting for transfers between devices  125 us (46%)
  blocking collectives  44.2 us (16%)
  starting transfers between devices  38.2 us (14%)
  matrix products  21.1 us (8%)
  local copies, waits for them, and re-layouts  17.6 us (6%)
  between operations  15.1 us (6%)
  other arithmetic  8.23 us (3%)
    psum x1, waiting for transfers between devices, section_run(): lax.psum(lax.psum((grads_space, grads_time), 'row'), 'frame')  45.6 us
    ppermute x3, waiting for transfers between devices, from_behind(): return lax.ppermute(block, axis, route)  28.2 us
    all_to_all x2, blocking collectives, section_run(): lax.all_to_all(to_blocks(incoming, frame_parts), 'frame', split_axis=1, c...  22.4 us
    all_to_all x2, blocking collectives, spatial_back(): lax.all_to_all(back_tiles, 'frame', split_axis=0, concat_axis=1, tiled=True)  21.8 us
    psum x1, waiting for transfers between devices, section_run(): lax.psum((grads_space, grads_time), 'row')  17.8 us
    all_to_all x2, waiting for transfers between devices, section_run(): lax.all_to_all(to_blocks(incoming, frame_parts), 'frame', split_axis=1, c...  13 us
    unnamed x52, local copies, waits for them, and re-layouts  11.1 us
    all_to_all x2, waiting for transfers between devices, spatial_back(): lax.all_to_all(back_tiles, 'frame', split_axis=0, concat_axis=1, tiled=True)  10.4 us
  transfers between devices with their start and end apart: 20, of which 13 were waited for; matrix products, arithmetic and copies ran while one was open for 7% of the time, Pallas kernels for 0%

profile of v1, /device:TPU:0, one launch (start us, length us, event | category | flops | bytes accessed | tf_op | source)
XLA Modules:
  0.0 269.7 jit_solution(678909533212383266)
XLA Ops:
  8.0 2.3 collective-permute-start
  11.6 1.7 copy.56
  13.3 5.8 %all-to-all-start = ((bf16[2,4,128,128]{3,2,0,1:T(8,128)(2,1)}), bf16[2,4,128,128]{3,2,0,1:T(8,128)(2,1)S(1)}, u32[]{:S(2)}, u32[]{:S(2)}) async-start(bf16[2,4,128,128]{3,2,0,1:T(8,128)(2,1)} %copy.56), calls=%async_computation | async-start | bytes 524288 | tf_op jit(solution)/shard_map/all_to_all | solution.py:121
  22.3 7.0 %all-to-all-done = bf16[2,4,128,128]{3,2,0,1:T(8,128)(2,1)S(1)} async-done(((bf16[2,4,128,128]{3,2,0,1:T(8,128)(2,1)}), bf16[2,4,128,128]{3,2,0,1:T(8,128)(2,1)S(1)}, u32[]{:S(2)}, u32[]{:S(2)}) %all-to-all-start) | async-done | bytes 262176 | tf_op jit(solution)/shard_map/all_to_all | solution.py:121
  31.6 3.4 %all-to-all-start.1 = ((bf16[8,1,128,128]{3,2,1,0:T(8,128)(2,1)}), bf16[8,1,128,128]{3,2,1,0:T(8,128)(2,1)S(1)}, u32[]{:S(2)}, u32[]{:S(2)}) async-start(bf16[8,1,128,128]{3,2,1,0:T(8,128)(2,1)} %bitcast.12), calls=%async_computation.1 | async-start | bytes 524288 | tf_op jit(solution)/shard_map/all_to_all | solution.py:81
  36.2 8.1 %all-to-all-done.1 = bf16[8,1,128,128]{3,2,1,0:T(8,128)(2,1)S(1)} async-done(((bf16[8,1,128,128]{3,2,1,0:T(8,128)(2,1)}), bf16[8,1,128,128]{3,2,1,0:T(8,128)(2,1)S(1)}, u32[]{:S(2)}, u32[]{:S(2)}) %all-to-all-start.1) | async-done | bytes 262176 | tf_op jit(solution)/shard_map/all_to_all | solution.py:81
  49.3 1.8 collective-permute-done.3
  55.8 9.0 %collective-permute-done.4 = bf16[2,8,64,128]{3,2,1,0:T(8,128)(2,1)S(1)} collective-permute-done((bf16[2,8,64,128]{3,2,1,0:T(8,128)(2,1)S(1)}, bf16[2,8,64,128]{3,2,1,0:T(8,128)(2,1)S(1)}, u32[]{:S(2)}, u32[]{:S(2)}) %collective-permute-start.4) | collective-permute-done | bytes 262176 | tf_op jit(solution)/shard_map/ppermute | solution.py:27
  64.8 11.0 %all_to_all.126 = bf16[2,4,128,128]{3,2,0,1:T(8,128)(2,1)S(1)} all-to-all(bf16[2,4,128,128]{3,2,0,1:T(8,128)(2,1)S(1)} %copy.61), channel_id=1, replica_groups=mesh['section'=4,'frame'=4,'row'=2] {'frame'}, dimensions={1} | all-to-all | bytes 524288 | tf_op jit(solution)/shard_map/all_to_all | solution.py:121
  76.6 10.9 %all_to_all.127 = bf16[8,1,128,128]{3,2,1,0:T(8,128)(2,1)S(1)} all-to-all(bf16[8,1,128,128]{3,2,1,0:T(8,128)(2,1)S(1)} %bitcast.558), channel_id=1, replica_groups=mesh['section'=4,'frame'=4,'row'=2] {'frame'}, dimensions={0} | all-to-all | bytes 524288 | tf_op jit(solution)/shard_map/all_to_all | solution.py:81
  96.9 9.6 %collective-permute-done.7 = bf16[2,8,64,128]{3,2,1,0:T(8,128)(2,1)S(1)} collective-permute-done((bf16[2,8,64,128]{3,2,1,0:T(8,128)(2,1)S(1)}, bf16[2,8,64,128]{3,2,1,0:T(8,128)(2,1)S(1)}, u32[]{:S(2)}, u32[]{:S(2)}) %collective-permute-start.7) | collective-permute-done | bytes 262176 | tf_op jit(solution)/shard_map/ppermute | solution.py:27
  106.5 11.3 %all_to_all.128 = bf16[2,4,128,128]{3,2,0,1:T(8,128)(2,1)S(1)} all-to-all(bf16[2,4,128,128]{3,2,0,1:T(8,128)(2,1)S(1)} %copy.66), channel_id=1, replica_groups=mesh['section'=4,'frame'=4,'row'=2] {'frame'}, dimensions={1} | all-to-all | bytes 524288 | tf_op jit(solution)/shard_map/all_to_all | solution.py:121
  118.7 10.9 %all_to_all.129 = bf16[8,1,128,128]{3,2,1,0:T(8,128)(2,1)S(1)} all-to-all(bf16[8,1,128,128]{3,2,1,0:T(8,128)(2,1)S(1)} %bitcast.559), channel_id=1, replica_groups=mesh['section'=4,'frame'=4,'row'=2] {'frame'}, dimensions={0} | all-to-all | bytes 524288 | tf_op jit(solution)/shard_map/all_to_all | solution.py:81
  139.6 9.6 %collective-permute-done.10 = bf16[2,8,64,128]{3,2,1,0:T(8,128)(2,1)S(1)} collective-permute-done((bf16[2,8,64,128]{3,2,1,0:T(8,128)(2,1)S(1)}, bf16[2,8,64,128]{3,2,1,0:T(8,128)(2,1)S(1)}, u32[]{:S(2)}, u32[]{:S(2)}) %collective-permute-start.10) | collective-permute-done | bytes 262176 | tf_op jit(solution)/shard_map/ppermute | solution.py:27
  150.0 3.4 %all-to-all-start.6 = ((bf16[2,4,128,128]{3,2,0,1:T(8,128)(2,1)}), bf16[2,4,128,128]{3,2,0,1:T(8,128)(2,1)S(1)}, u32[]{:S(2)}, u32[]{:S(2)}) async-start(bf16[2,4,128,128]{3,2,0,1:T(8,128)(2,1)} %copy.71), calls=%async_computation.6 | async-start | bytes 524288 | tf_op jit(solution)/shard_map/all_to_all | solution.py:121
  154.4 1.9 multiply_convert_fusion
  156.3 6.1 %all-to-all-done.6 = bf16[2,4,128,128]{3,2,0,1:T(8,128)(2,1)S(1)} async-done(((bf16[2,4,128,128]{3,2,0,1:T(8,128)(2,1)}), bf16[2,4,128,128]{3,2,0,1:T(8,128)(2,1)S(1)}, u32[]{:S(2)}, u32[]{:S(2)}) %all-to-all-start.6) | async-done | bytes 262176 | tf_op jit(solution)/shard_map/all_to_all | solution.py:121
  162.4 4.1 %all-to-all-start.8 = ((bf16[2,4,128,128]{2,3,0,1:T(8,128)(2,1)}), bf16[2,4,128,128]{2,3,0,1:T(8,128)(2,1)}, u32[]{:S(2)}, u32[]{:S(2)}) async-start(bf16[2,4,128,128]{2,3,0,1:T(8,128)(2,1)} %multiply_convert_fusion), calls=%async_computation.8 | async-start | bytes 524288 | tf_op jit(solution)/shard_map/all_to_all | solution.py:113
  168.1 5.4 %all-to-all-done.8 = bf16[2,4,128,128]{2,3,0,1:T(8,128)(2,1)} async-done(((bf16[2,4,128,128]{2,3,0,1:T(8,128)(2,1)}), bf16[2,4,128,128]{2,3,0,1:T(8,128)(2,1)}, u32[]{:S(2)}, u32[]{:S(2)}) %all-to-all-start.8) | async-done | bytes 262176 | tf_op jit(solution)/shard_map/all_to_all | solution.py:113
  173.5 3.4 %all-to-all-start.7 = ((bf16[8,1,128,128]{3,2,1,0:T(8,128)(2,1)}), bf16[8,1,128,128]{3,2,1,0:T(8,128)(2,1)S(1)}, u32[]{:S(2)}, u32[]{:S(2)}) async-start(bf16[8,1,128,128]{3,2,1,0:T(8,128)(2,1)} %bitcast.548), calls=%async_computation.7 | async-start | bytes 524288 | tf_op jit(solution)/shard_map/all_to_all | solution.py:81
  181.4 2.3 all-to-all-done.7
  194.6 17.8 %all-reduce.17.cloned.1.call-done = (f32[3,3,128,128]{3,2,1,0:T(8,128)}, f32[3,128,128]{2,1,0:T(8,128)}) async-done(((f32[3,3,128,128]{3,2,1,0:T(8,128)}, f32[3,128,128]{2,1,0:T(8,128)}), (f32[3,3,128,128]{3,2,1,0:T(8,128)}, f32[3,128,128]{2,1,0:T(8,128)})) %all-reduce.17.cloned.1.call-update) | async-done | bytes 786448 | tf_op jit(solution)/shard_map/psum | solution.py:160
  214.6 45.6 %all-reduce.15.cloned.1.call-done = (f32[1,3,3,128,128]{4,3,2,1,0:T(8,128)}, f32[1,3,128,128]{3,2,1,0:T(8,128)}) async-done(((f32[1,3,3,128,128]{4,3,2,1,0:T(8,128)}, f32[1,3,128,128]{3,2,1,0:T(8,128)}), (f32[1,3,3,128,128]{4,3,2,1,0:T(8,128)}, f32[1,3,128,128]{3,2,1,0:T(8,128)})) %all-reduce.15.cloned.1.call-update) | async-done | bytes 786448 | tf_op jit(solution)/shard_map/psum | solution.py:160
  260.2 2.0 copy.100
  (199 shorter events, 60.3 us)
Async XLA Ops:
  8.0 11.2 %collective-permute-start = (bf16[2,1,64,128]{3,2,1,0:T(8,128)(2,1)S(1)}, bf16[2,1,64,128]{3,2,1,0:T(8,128)(2,1)S(1)}, u32[]{:S(2)}, u32[]{:S(2)}) collective-permute-start(bf16[2,1,64,128]{3,2,1,0:T(8,128)(2,1)S(1)} %get-tuple-element.63), channel_id=1, source_target_pairs={{0,1},{2,3},{4,5},{6,7},{8,9},{10,11},{12,13},{14,15},{16,17},{18,... | collective-permute-start | bytes 98312 | tf_op jit(solution)/shard_map/ppermute | solution.py:15
  10.3 8.8 %collective-permute-start.1 = (bf16[2,1,64,128]{3,2,1,0:T(8,128)(2,1)S(1)}, bf16[2,1,64,128]{3,2,1,0:T(8,128)(2,1)S(1)}, u32[]{:S(2)}, u32[]{:S(2)}) collective-permute-start(bf16[2,1,64,128]{3,2,1,0:T(8,128)(2,1)S(1)} %get-tuple-element.64), channel_id=1, source_target_pairs={{1,0},{3,2},{5,4},{7,6},{9,8},{11,10},{13,12},{15,14},{17,16},{19,... | collective-permute-start | bytes 98312 | tf_op jit(solution)/shard_map/ppermute | solution.py:17
  13.3 5.8 %copy-start.1 = (bf16[1,2,8,64,128]{4,3,2,1,0:T(8,128)(2,1)S(1)}, bf16[1,2,8,64,128]{4,3,2,1,0:T(8,128)(2,1)}, u32[]{:S(2)}) copy-start(bf16[1,2,8,64,128]{4,3,2,1,0:T(8,128)(2,1)} %param.4) | copy-start | bytes 786436
  13.3 16.0 %all-to-all-start = ((bf16[2,4,128,128]{3,2,0,1:T(8,128)(2,1)}), bf16[2,4,128,128]{3,2,0,1:T(8,128)(2,1)S(1)}, u32[]{:S(2)}, u32[]{:S(2)}) async-start(bf16[2,4,128,128]{3,2,0,1:T(8,128)(2,1)} %copy.56), calls=%async_computation | async-start | bytes 524288 | tf_op jit(solution)/shard_map/all_to_all | solution.py:121
  31.6 12.7 %all-to-all-start.1 = ((bf16[8,1,128,128]{3,2,1,0:T(8,128)(2,1)}), bf16[8,1,128,128]{3,2,1,0:T(8,128)(2,1)S(1)}, u32[]{:S(2)}, u32[]{:S(2)}) async-start(bf16[8,1,128,128]{3,2,1,0:T(8,128)(2,1)} %bitcast.12), calls=%async_computation.1 | async-start | bytes 524288 | tf_op jit(solution)/shard_map/all_to_all | solution.py:81
  46.7 2.6 collective-permute-start.2
  48.0 3.1 %collective-permute-start.3 = (bf16[2,1,64,128]{3,2,1,0:T(8,128)(2,1)S(1)}, bf16[2,1,64,128]{3,2,1,0:T(8,128)(2,1)S(1)}, u32[]{:S(2)}, u32[]{:S(2)}) collective-permute-start(bf16[2,1,64,128]{3,2,1,0:T(8,128)(2,1)S(1)} %get-tuple-element.60), channel_id=1, source_target_pairs={{1,0},{3,2},{5,4},{7,6},{9,8},{11,10},{13,12},{15,14},{17,16},{19,... | collective-permute-start | bytes 98312 | tf_op jit(solution)/shard_map/ppermute | solution.py:17
  54.5 10.3 %copy-start.10 = (bf16[2,8,64,128]{3,2,1,0:T(8,128)(2,1)}, bf16[2,8,64,128]{3,2,1,0:T(8,128)(2,1)S(1)}, u32[]{:S(2)}) copy-start(bf16[2,8,64,128]{3,2,1,0:T(8,128)(2,1)S(1)} %add_convert_fusion.3) | copy-start | bytes 786436
  54.5 10.3 %collective-permute-start.4 = (bf16[2,8,64,128]{3,2,1,0:T(8,128)(2,1)S(1)}, bf16[2,8,64,128]{3,2,1,0:T(8,128)(2,1)S(1)}, u32[]{:S(2)}, u32[]{:S(2)}) collective-permute-start(bf16[2,8,64,128]{3,2,1,0:T(8,128)(2,1)S(1)} %add_convert_fusion.3), channel_id=1, source_target_pairs={{8,0},{16,8},{24,16},{9,1},{17,9},{25,17},{10,2},{18,10},{26,18},{... | collective-permute-start | bytes 786440 | tf_op jit(solution)/shard_map/ppermute | solution.py:27
  88.6 2.8 %collective-permute-start.5 = (bf16[2,1,64,128]{3,2,1,0:T(8,128)(2,1)S(1)}, bf16[2,1,64,128]{3,2,1,0:T(8,128)(2,1)S(1)}, u32[]{:S(2)}, u32[]{:S(2)}) collective-permute-start(bf16[2,1,64,128]{3,2,1,0:T(8,128)(2,1)S(1)} %get-tuple-element.53), channel_id=1, source_target_pairs={{0,1},{2,3},{4,5},{6,7},{8,9},{10,11},{12,13},{14,15},{16,17},{18,... | collective-permute-start | bytes 98312 | tf_op jit(solution)/shard_map/ppermute | solution.py:15
  89.9 3.1 %collective-permute-start.6 = (bf16[2,1,64,128]{3,2,1,0:T(8,128)(2,1)S(1)}, bf16[2,1,64,128]{3,2,1,0:T(8,128)(2,1)S(1)}, u32[]{:S(2)}, u32[]{:S(2)}) collective-permute-start(bf16[2,1,64,128]{3,2,1,0:T(8,128)(2,1)S(1)} %get-tuple-element.54), channel_id=1, source_target_pairs={{1,0},{3,2},{5,4},{7,6},{9,8},{11,10},{13,12},{15,14},{17,16},{19,... | collective-permute-start | bytes 98312 | tf_op jit(solution)/shard_map/ppermute | solution.py:17
  95.6 10.9 %copy-start.12 = (bf16[2,8,64,128]{3,2,1,0:T(8,128)(2,1)}, bf16[2,8,64,128]{3,2,1,0:T(8,128)(2,1)S(1)}, u32[]{:S(2)}) copy-start(bf16[2,8,64,128]{3,2,1,0:T(8,128)(2,1)S(1)} %add_convert_fusion.2) | copy-start | bytes 786436
  95.6 10.9 %collective-permute-start.7 = (bf16[2,8,64,128]{3,2,1,0:T(8,128)(2,1)S(1)}, bf16[2,8,64,128]{3,2,1,0:T(8,128)(2,1)S(1)}, u32[]{:S(2)}, u32[]{:S(2)}) collective-permute-start(bf16[2,8,64,128]{3,2,1,0:T(8,128)(2,1)S(1)} %add_convert_fusion.2), channel_id=1, source_target_pairs={{8,0},{16,8},{24,16},{9,1},{17,9},{25,17},{10,2},{18,10},{26,18},{... | collective-permute-start | bytes 786440 | tf_op jit(solution)/shard_map/ppermute | solution.py:27
  130.6 2.8 %collective-permute-start.8 = (bf16[2,1,64,128]{3,2,1,0:T(8,128)(2,1)S(1)}, bf16[2,1,64,128]{3,2,1,0:T(8,128)(2,1)S(1)}, u32[]{:S(2)}, u32[]{:S(2)}) collective-permute-start(bf16[2,1,64,128]{3,2,1,0:T(8,128)(2,1)S(1)} %get-tuple-element.47), channel_id=1, source_target_pairs={{0,1},{2,3},{4,5},{6,7},{8,9},{10,11},{12,13},{14,15},{16,17},{18,... | collective-permute-start | bytes 98312 | tf_op jit(solution)/shard_map/ppermute | solution.py:15
  131.9 3.1 %collective-permute-start.9 = (bf16[2,1,64,128]{3,2,1,0:T(8,128)(2,1)S(1)}, bf16[2,1,64,128]{3,2,1,0:T(8,128)(2,1)S(1)}, u32[]{:S(2)}, u32[]{:S(2)}) collective-permute-start(bf16[2,1,64,128]{3,2,1,0:T(8,128)(2,1)S(1)} %get-tuple-element.48), channel_id=1, source_target_pairs={{1,0},{3,2},{5,4},{7,6},{9,8},{11,10},{13,12},{15,14},{17,16},{19,... | collective-permute-start | bytes 98312 | tf_op jit(solution)/shard_map/ppermute | solution.py:17
  138.3 10.9 %collective-permute-start.10 = (bf16[2,8,64,128]{3,2,1,0:T(8,128)(2,1)S(1)}, bf16[2,8,64,128]{3,2,1,0:T(8,128)(2,1)S(1)}, u32[]{:S(2)}, u32[]{:S(2)}) collective-permute-start(bf16[2,8,64,128]{3,2,1,0:T(8,128)(2,1)S(1)} %add_convert_fusion.1), channel_id=1, source_target_pairs={{8,0},{16,8},{24,16},{9,1},{17,9},{25,17},{10,2},{18,10},{26,18},{... | collective-permute-start | bytes 786440 | tf_op jit(solution)/shard_map/ppermute | solution.py:27
  150.0 12.4 %all-to-all-start.6 = ((bf16[2,4,128,128]{3,2,0,1:T(8,128)(2,1)}), bf16[2,4,128,128]{3,2,0,1:T(8,128)(2,1)S(1)}, u32[]{:S(2)}, u32[]{:S(2)}) async-start(bf16[2,4,128,128]{3,2,0,1:T(8,128)(2,1)} %copy.71), calls=%async_computation.6 | async-start | bytes 524288 | tf_op jit(solution)/shard_map/all_to_all | solution.py:121
  162.4 11.1 %all-to-all-start.8 = ((bf16[2,4,128,128]{2,3,0,1:T(8,128)(2,1)}), bf16[2,4,128,128]{2,3,0,1:T(8,128)(2,1)}, u32[]{:S(2)}, u32[]{:S(2)}) async-start(bf16[2,4,128,128]{2,3,0,1:T(8,128)(2,1)} %multiply_convert_fusion), calls=%async_computation.8 | async-start | bytes 524288 | tf_op jit(solution)/shard_map/all_to_all | solution.py:113
  173.5 10.2 %all-to-all-start.7 = ((bf16[8,1,128,128]{3,2,1,0:T(8,128)(2,1)}), bf16[8,1,128,128]{3,2,1,0:T(8,128)(2,1)S(1)}, u32[]{:S(2)}, u32[]{:S(2)}) async-start(bf16[8,1,128,128]{3,2,1,0:T(8,128)(2,1)} %bitcast.548), calls=%async_computation.7 | async-start | bytes 524288 | tf_op jit(solution)/shard_map/all_to_all | solution.py:81
  176.9 35.5 %all-reduce.17.cloned.1.call-start = ((), (), s32[]{:S(2)}) async-start(), calls=%async_computation.10 | async-start | bytes 1572864 | tf_op jit(solution)/shard_map/psum | solution.py:160
  187.6 2.6 copy-start.24
  187.6 4.9 %collective-permute-start.11 = (bf16[2,1,64,128]{3,2,1,0:T(8,128)(2,1)S(1)}, bf16[2,1,64,128]{3,2,1,0:T(8,128)(2,1)S(1)}, u32[]{:S(2)}, u32[]{:S(2)}) collective-permute-start(bf16[2,1,64,128]{3,2,1,0:T(8,128)(2,1)S(1)} %get-tuple-element.41), channel_id=1, source_target_pairs={{0,1},{2,3},{4,5},{6,7},{8,9},{10,11},{12,13},{14,15},{16,17},{18,... | collective-permute-start | bytes 98312 | tf_op jit(solution)/shard_map/ppermute | solution.py:15
  188.9 3.6 %collective-permute-start.12 = (bf16[2,1,64,128]{3,2,1,0:T(8,128)(2,1)S(1)}, bf16[2,1,64,128]{3,2,1,0:T(8,128)(2,1)S(1)}, u32[]{:S(2)}, u32[]{:S(2)}) collective-permute-start(bf16[2,1,64,128]{3,2,1,0:T(8,128)(2,1)S(1)} %get-tuple-element.42), channel_id=1, source_target_pairs={{1,0},{3,2},{5,4},{7,6},{9,8},{11,10},{13,12},{15,14},{17,16},{19,... | collective-permute-start | bytes 98312 | tf_op jit(solution)/shard_map/ppermute | solution.py:17
  192.5 67.7 %all-reduce.15.cloned.1.call-start = ((), (), s32[]{:S(2)}) async-start(), calls=%async_computation.9 | async-start | bytes 1572864 | tf_op jit(solution)/shard_map/psum | solution.py:160
  (21 other events, 21.3 us)
Sparse Core Ops, SparseCore 0:
  192.6 19.7 all-reduce.16
  214.9 45.2 all-reduce.14
